TPU v7x, 32 devices: a whole 2x2x4 slice. The times are simulated.
32 devices in a mesh: rows: 16 (over z, y, core), maze: 2 (over x).
Axes of the slice: x: 2, y: 2, z: 4, core: 2. Of those that a mesh axis runs over, the one named last changes fastest.
Arguments:
- maze_walls: int32 [2, 128, 256], P('maze', 'rows'), may hold values 0 or 1
- goal_cell: int32 [2, 2], P('maze'), may hold values from 0 to 127
- start_hidden: bfloat16 [2, 32, 128, 256], P('maze', None, 'rows'), may hold values from -0.8984375 to 0.8984375
- start_cell: float32 [2, 32, 128, 256], P('maze', None, 'rows'), may hold values from -4 to 4
- cotangent: bfloat16 [2, 3, 32, 128, 256], P('maze', None, None, 'rows'), may hold values from -6 to 6
- gate_weights: bfloat16 [73728], P(('rows', 'maze')), may hold values from -0.25 to 0.25
- embed_table: float32 [3, 32], replicated, may hold values from -4 to 4
Outputs:
- grad_weights: float32 [73728], P(('rows', 'maze'))
- grad_table: float32 [3, 32], replicated
- grad_hidden: float32 [2, 32, 128, 256], P('maze', None, 'rows')
- grad_cell: float32 [2, 32, 128, 256], P('maze', None, 'rows')
Inputs may be any that keep to these rules, and one draw needn't show every extreme that they name: `maze_walls`: 0 for open cells, 1 for walls. `goal_cell`: goal row and column inside the grid.
All inputs are finite; a program needn't handle non-finite values. No bound on the sum of `maze_walls` on one device may be relied on, other than what follows from the above.
Results may differ from a plain program's by a relative error of at most 0.0044.
Values may be sent and summed in bfloat16 or wider, within the bound.
A program may use at most 64 MiB of HBM per device.

v0:
```python
import math
import jax
import jax.numpy as jnp
from jax import lax
from jax.sharding import PartitionSpec as P

goal_reach = 64.0


def extended(cells, sides, width):
    for axis, dim in sides:
        count = lax.axis_size(axis)
        ends = count - 1
        head = lax.slice_in_dim(cells, 0, width, axis=dim)
        tail = lax.slice_in_dim(cells, cells.shape[dim] - width, cells.shape[dim], axis=dim)
        cells = jnp.concatenate(
            [
                lax.ppermute(tail, axis, [(i, (i + 1) % count) for i in range(ends)]),
                cells,
                lax.ppermute(head, axis, [((i + 1) % count, i) for i in range(ends)]),
            ],
            axis=dim,
        )
    return cells


def tap_offsets():
    return [(row_off, col_off) for row_off in (-1, 0, 1) for col_off in (-1, 0, 1)]


def gate_conv(padded, kernel, row_count, col_count):
    summed = None
    for tap_index, (row_off, col_off) in enumerate(tap_offsets()):
        window = padded[
            :, 1 + row_off : 1 + row_off + row_count, 1 + col_off : 1 + col_off + col_count
        ]
        tap_term = jnp.einsum(
            "gc,crq->grq", kernel[tap_index], window, preferred_element_type=jnp.float32
        )
        summed = tap_term if summed is None else summed + tap_term
    return summed


def weight_grads(gate_grad, padded, row_count, col_count):
    pieces = []
    for row_off, col_off in tap_offsets():
        window = padded[
            :, 1 + row_off : 1 + row_off + row_count, 1 + col_off : 1 + col_off + col_count
        ]
        pieces.append(
            jnp.einsum("grq,crq->gc", gate_grad, window, preferred_element_type=jnp.float32)
        )
    return jnp.stack(pieces)


def per_device(
    maze_walls, goal_cell, start_hidden, start_cell, cotangent, gate_weights, embed_table
):
    row_count = maze_walls.shape[1]
    col_count = maze_walls.shape[2]
    hidden_width = start_hidden.shape[1]
    input_width = embed_table.shape[1]
    channels = input_width + hidden_width
    step_count = cotangent.shape[1]
    gathered = lax.all_gather(gate_weights, ("rows", "maze"), axis=0, tiled=True)
    kernel = gathered.reshape(9, 4 * hidden_width, channels)
    first_row = lax.axis_index("rows") * row_count
    row_pos = first_row + lax.broadcasted_iota(jnp.int32, (row_count, col_count), 0)
    col_pos = lax.broadcasted_iota(jnp.int32, (row_count, col_count), 1)
    distance = (jnp.abs(row_pos - goal_cell[0, 0]) + jnp.abs(col_pos - goal_cell[0, 1])).astype(
        jnp.float32
    )
    goal_bump = jnp.exp(-distance / goal_reach)
    wall_mask = (maze_walls[0] == 1).astype(jnp.float32)
    inputs = (
        embed_table[0][:, None, None] * (1.0 - wall_mask)
        + embed_table[1][:, None, None] * wall_mask
        + embed_table[2][:, None, None] * goal_bump
    ).astype(jnp.bfloat16)
    input_ext = extended(inputs, (("rows", 1),), 1)
    hidden = start_hidden[0]
    cell_state = start_cell[0]
    stored = []
    for step_index in range(step_count):
        hidden_ext = extended(hidden, (("rows", 1),), 1)
        padded = jnp.pad(jnp.concatenate([input_ext, hidden_ext], axis=0), ((0, 0), (0, 0), (1, 1)))
        pre_gate = gate_conv(padded, kernel, row_count, col_count)
        in_gate = jax.nn.sigmoid(pre_gate[:hidden_width])
        forget_gate = jax.nn.sigmoid(pre_gate[hidden_width : 2 * hidden_width] + 1.0)
        out_gate = jax.nn.sigmoid(pre_gate[2 * hidden_width : 3 * hidden_width])
        cand_gate = jnp.tanh(pre_gate[3 * hidden_width :])
        new_cell = forget_gate * cell_state + in_gate * cand_gate
        squash = jnp.tanh(new_cell)
        stored.append((padded, cell_state, in_gate, forget_gate, out_gate, cand_gate, squash))
        hidden = (out_gate * squash).astype(jnp.bfloat16)
        cell_state = new_cell
    carry_hidden = jnp.zeros((hidden_width, row_count, col_count), jnp.float32)
    carry_cell = jnp.zeros((hidden_width, row_count, col_count), jnp.float32)
    kernel_acc = jnp.zeros((9, 4 * hidden_width, channels), jnp.float32)
    input_acc = jnp.zeros((input_width, row_count, col_count), jnp.float32)
    for step_index in reversed(range(step_count)):
        padded, prev_cell, in_gate, forget_gate, out_gate, cand_gate, squash = stored[step_index]
        hid_grad = cotangent[0, step_index].astype(jnp.float32) + carry_hidden
        cell_grad = carry_cell + hid_grad * out_gate * (1.0 - squash * squash)
        gate_grad = jnp.concatenate(
            [
                cell_grad * cand_gate * in_gate * (1.0 - in_gate),
                cell_grad * prev_cell * forget_gate * (1.0 - forget_gate),
                hid_grad * squash * out_gate * (1.0 - out_gate),
                cell_grad * in_gate * (1.0 - cand_gate * cand_gate),
            ],
            axis=0,
        ).astype(jnp.bfloat16)
        step_kernel = weight_grads(gate_grad, padded, row_count, col_count)
        kernel_acc = kernel_acc + step_kernel
        grad_ext = extended(gate_grad, (("rows", 1),), 1)
        grad_padded = jnp.pad(grad_ext, ((0, 0), (0, 0), (1, 1)))
        stack_grad = None
        for tap_index, (row_off, col_off) in enumerate(tap_offsets()):
            window = grad_padded[
                :, 1 - row_off : 1 - row_off + row_count, 1 - col_off : 1 - col_off + col_count
            ]
            tap_term = jnp.einsum(
                "gc,grq->crq", kernel[tap_index], window, preferred_element_type=jnp.float32
            )
            stack_grad = tap_term if stack_grad is None else stack_grad + tap_term
        input_acc = input_acc + stack_grad[:input_width]
        carry_hidden = stack_grad[input_width:]
        carry_cell = cell_grad * forget_gate
    scale = 1.0 / math.sqrt(
        lax.axis_size("maze") * lax.axis_size("rows") * row_count * col_count * step_count
    )
    grad_weights = (
        lax.psum_scatter(kernel_acc.reshape(-1), ("rows", "maze"), scatter_dimension=0, tiled=True)
        * scale
    )
    pieces = jnp.stack(
        [
            jnp.sum(input_acc * (1.0 - wall_mask), axis=(1, 2)),
            jnp.sum(input_acc * wall_mask, axis=(1, 2)),
            jnp.sum(input_acc * goal_bump, axis=(1, 2)),
        ]
    )
    grad_table = lax.psum(pieces, ("rows", "maze")) * scale
    return (grad_weights, grad_table, carry_hidden[None], carry_cell[None])


def solution(mesh):
    return jax.shard_map(
        per_device,
        mesh=mesh,
        in_specs=(
            P("maze", "rows", None),
            P("maze", None),
            P("maze", None, "rows", None),
            P("maze", None, "rows", None),
            P("maze", None, None, "rows", None),
            P(("rows", "maze")),
            P(),
        ),
        out_specs=(
            P(("rows", "maze")),
            P(),
            P("maze", None, "rows", None),
            P("maze", None, "rows", None),
        ),
        check_vma=False,
    )
```

profile of v0, /device:TPU:8, one launch (start us, length us, event | category | flops | bytes accessed | tf_op | source)
XLA Modules:
  0.0 296.0 jit_solution(9705465087397272263)
XLA Ops:
  7.2 1.3 fusion.286
  11.6 1.9 collective-permute-start
  13.5 4.5 %collective-permute-start.1 = (bf16[32,1,256]{2,0,1:T(8,128)(2,1)S(1)}, bf16[32,1,256]{2,0,1:T(8,128)(2,1)S(1)}, u32[]{:S(2)}, u32[]{:S(2)}) collective-permute-start(bf16[32,1,256]{2,0,1:T(8,128)(2,1)S(1)} %get-tuple-element.67), channel_id=1, source_target_pairs={{2,0},{4,2},{6,4},{8,6},{10,8},{12,10},{14,12},{16,14},{18,16},{20... | collective-permute-start | bytes 49160 | tf_op jit(solution)/shard_map/ppermute | solution.py:20
  19.0 1.9 collective-permute-start.2
  20.9 4.5 %collective-permute-start.3 = (bf16[32,1,256]{2,0,1:T(8,128)(2,1)S(1)}, bf16[32,1,256]{2,0,1:T(8,128)(2,1)S(1)}, u32[]{:S(2)}, u32[]{:S(2)}) collective-permute-start(bf16[32,1,256]{2,0,1:T(8,128)(2,1)S(1)} %get-tuple-element.69), channel_id=1, source_target_pairs={{2,0},{4,2},{6,4},{8,6},{10,8},{12,10},{14,12},{16,14},{18,16},{20... | collective-permute-start | bytes 49160 | tf_op jit(solution)/shard_map/ppermute | solution.py:20
  26.2 53.3 %all-gather = bf16[32,1,2304]{2,1,0:T(2,128)(2,1)S(1)} all-gather(bf16[1,1,2304]{2,1,0:T(2,128)(2,1)S(1)} %reshape.144), channel_id=1, replica_groups=mesh['rows'=16,'maze'=2] {'rows','maze'}, dimensions={0}, use_global_device_ids=true | all-gather | bytes 152064 | tf_op jit(solution)/shard_map/all_gather | solution.py:65
  85.4 1.9 collective-permute-start.4
  87.4 6.4 %collective-permute-start.5 = (bf16[32,1,256]{2,0,1:T(8,128)(2,1)S(1)}, bf16[32,1,256]{2,0,1:T(8,128)(2,1)S(1)}, u32[]{:S(2)}, u32[]{:S(2)}) collective-permute-start(bf16[32,1,256]{2,0,1:T(8,128)(2,1)S(1)} %get-tuple-element.65), channel_id=1, source_target_pairs={{2,0},{4,2},{6,4},{8,6},{10,8},{12,10},{14,12},{16,14},{18,16},{20... | collective-permute-start | bytes 49160 | tf_op jit(solution)/shard_map/ppermute | solution.py:20
  93.8 1.4 collective-permute-done.5
  98.3 0.9 multiply_convert_fusion.10
  99.2 1.3 fusion.282
  100.6 1.9 collective-permute-start.6
  102.5 4.7 %collective-permute-start.7 = (bf16[32,1,256]{2,0,1:T(8,128)(2,1)}, bf16[32,1,256]{2,0,1:T(8,128)(2,1)}, u32[]{:S(2)}, u32[]{:S(2)}) collective-permute-start(bf16[32,1,256]{2,0,1:T(8,128)(2,1)} %get-tuple-element.63), channel_id=1, source_target_pairs={{2,0},{4,2},{6,4},{8,6},{10,8},{12,10},{14,12},{16,14},{18,16},{20... | collective-permute-start | bytes 49160 | tf_op jit(solution)/shard_map/ppermute | solution.py:20
  108.8 0.9 maximum_maximum_fusion.2
  109.8 1.1 fusion.180
  116.3 1.9 collective-permute-start.8
  118.3 6.7 %collective-permute-start.9 = (bf16[128,1,256]{2,0,1:T(8,128)(2,1)S(1)}, bf16[128,1,256]{2,0,1:T(8,128)(2,1)S(1)}, u32[]{:S(2)}, u32[]{:S(2)}) collective-permute-start(bf16[128,1,256]{2,0,1:T(8,128)(2,1)S(1)} %get-tuple-element.49), channel_id=1, source_target_pairs={{2,0},{4,2},{6,4},{8,6},{10,8},{12,10},{14,12},{16,14},{18,16},{20... | collective-permute-start | bytes 196616 | tf_op jit(solution)/shard_map/ppermute | solution.py:20
  133.2 1.9 collective-permute-start.10
  135.1 4.6 %collective-permute-start.11 = (bf16[128,1,256]{2,0,1:T(8,128)(2,1)S(1)}, bf16[128,1,256]{2,0,1:T(8,128)(2,1)S(1)}, u32[]{:S(2)}, u32[]{:S(2)}) collective-permute-start(bf16[128,1,256]{2,0,1:T(8,128)(2,1)S(1)} %get-tuple-element.47), channel_id=1, source_target_pairs={{2,0},{4,2},{6,4},{8,6},{10,8},{12,10},{14,12},{16,14},{18,16},{20... | collective-permute-start | bytes 196616 | tf_op jit(solution)/shard_map/ppermute | solution.py:20
  148.1 1.9 collective-permute-start.12
  150.0 4.8 %collective-permute-start.13 = (bf16[128,1,256]{2,0,1:T(8,128)(2,1)S(1)}, bf16[128,1,256]{2,0,1:T(8,128)(2,1)S(1)}, u32[]{:S(2)}, u32[]{:S(2)}) collective-permute-start(bf16[128,1,256]{2,0,1:T(8,128)(2,1)S(1)} %get-tuple-element.45), channel_id=1, source_target_pairs={{2,0},{4,2},{6,4},{8,6},{10,8},{12,10},{14,12},{16,14},{18,16},{20... | collective-permute-start | bytes 196616 | tf_op jit(solution)/shard_map/ppermute | solution.py:20
  165.7 39.5 %psum.7 = f32[3,32]{1,0:T(4,128)S(1)} all-reduce(f32[3,32]{1,0:T(4,128)S(1)} %pad_maximum_fusion.10), channel_id=1, replica_groups=mesh['rows'=16,'maze'=2] {'rows','maze'}, use_global_device_ids=true, to_apply=%region_4.5 | all-reduce | flops 96 | bytes 768 | tf_op jit(solution)/shard_map/psum | solution.py:144
  205.8 81.9 %all-reduce.9.cloned.1.call-done = f32[73728]{0:T(1024)} async-done(((f32[73728]{0:T(1024)}), f32[73728]{0:T(1024)}) %all-reduce.9.cloned.1.call-update) | async-done | bytes 294928
  287.7 1.4 dynamic-slice_multiply_fusion
  (202 shorter events, 48.1 us)
Async XLA Ops:
  7.2 280.6 %all-reduce.9.cloned.1.call-start = ((), (), s32[]{:S(2)}) async-start(), calls=%async_computation | async-start | bytes 589824
  10.7 14.8 %copy-start.25 = (f32[8,256]{1,0:T(8,128)}, f32[8,256]{1,0:T(8,128)S(1)}, u32[]{:S(2)}) copy-start(f32[8,256]{1,0:T(8,128)S(1)} %get-tuple-element.30) | copy-start | bytes 24580
  10.7 14.8 %copy-start.23 = (f32[8,256]{1,0:T(8,128)}, f32[8,256]{1,0:T(8,128)S(1)}, u32[]{:S(2)}) copy-start(f32[8,256]{1,0:T(8,128)S(1)} %convert_bitcast_fusion) | copy-start | bytes 24580
  11.4 14.1 %copy-start.27 = (f32[8,256]{1,0:T(8,128)}, f32[8,256]{1,0:T(8,128)S(1)}, u32[]{:S(2)}) copy-start(f32[8,256]{1,0:T(8,128)S(1)} %multiply_exponential_fusion) | copy-start | bytes 24580
  11.6 69.8 %collective-permute-start = (bf16[32,1,256]{2,0,1:T(8,128)(2,1)S(1)}, bf16[32,1,256]{2,0,1:T(8,128)(2,1)S(1)}, u32[]{:S(2)}, u32[]{:S(2)}) collective-permute-start(bf16[32,1,256]{2,0,1:T(8,128)(2,1)S(1)} %get-tuple-element.66), channel_id=1, source_target_pairs={{0,2},{2,4},{4,6},{6,8},{8,10},{10,12},{12,14},{14,16},{16,18},{18... | collective-permute-start | bytes 49160 | tf_op jit(solution)/shard_map/ppermute | solution.py:18
  13.5 67.9 %collective-permute-start.1 = (bf16[32,1,256]{2,0,1:T(8,128)(2,1)S(1)}, bf16[32,1,256]{2,0,1:T(8,128)(2,1)S(1)}, u32[]{:S(2)}, u32[]{:S(2)}) collective-permute-start(bf16[32,1,256]{2,0,1:T(8,128)(2,1)S(1)} %get-tuple-element.67), channel_id=1, source_target_pairs={{2,0},{4,2},{6,4},{8,6},{10,8},{12,10},{14,12},{16,14},{18,16},{20... | collective-permute-start | bytes 49160 | tf_op jit(solution)/shard_map/ppermute | solution.py:20
  19.0 62.4 %collective-permute-start.2 = (bf16[32,1,256]{2,0,1:T(8,128)(2,1)S(1)}, bf16[32,1,256]{2,0,1:T(8,128)(2,1)S(1)}, u32[]{:S(2)}, u32[]{:S(2)}) collective-permute-start(bf16[32,1,256]{2,0,1:T(8,128)(2,1)S(1)} %get-tuple-element.68), channel_id=1, source_target_pairs={{0,2},{2,4},{4,6},{6,8},{8,10},{10,12},{12,14},{14,16},{16,18},{18... | collective-permute-start | bytes 49160 | tf_op jit(solution)/shard_map/ppermute | solution.py:18
  20.9 60.5 %collective-permute-start.3 = (bf16[32,1,256]{2,0,1:T(8,128)(2,1)S(1)}, bf16[32,1,256]{2,0,1:T(8,128)(2,1)S(1)}, u32[]{:S(2)}, u32[]{:S(2)}) collective-permute-start(bf16[32,1,256]{2,0,1:T(8,128)(2,1)S(1)} %get-tuple-element.69), channel_id=1, source_target_pairs={{2,0},{4,2},{6,4},{8,6},{10,8},{12,10},{14,12},{16,14},{18,16},{20... | collective-permute-start | bytes 49160 | tf_op jit(solution)/shard_map/ppermute | solution.py:20
  80.8 16.8 %copy-start.7 = (bf16[128,64]{1,0:T(8,128)(2,1)}, bf16[128,64]{1,0:T(8,128)(2,1)S(1)}, u32[]{:S(2)}) copy-start(bf16[128,64]{1,0:T(8,128)(2,1)S(1)} %slice.531) | copy-start | bytes 49156
  81.0 15.6 %copy-start.9 = (bf16[128,64]{1,0:T(8,128)(2,1)}, bf16[128,64]{1,0:T(8,128)(2,1)S(1)}, u32[]{:S(2)}) copy-start(bf16[128,64]{1,0:T(8,128)(2,1)S(1)} %slice.522) | copy-start | bytes 49156
  81.2 14.7 %copy-start = (bf16[128,64]{1,0:T(8,128)(2,1)}, bf16[128,64]{1,0:T(8,128)(2,1)S(1)}, u32[]{:S(2)}) copy-start(bf16[128,64]{1,0:T(8,128)(2,1)S(1)} %slice.516) | copy-start | bytes 49156
  81.4 13.8 %copy-start.2 = (bf16[128,64]{1,0:T(8,128)(2,1)}, bf16[128,64]{1,0:T(8,128)(2,1)S(1)}, u32[]{:S(2)}) copy-start(bf16[128,64]{1,0:T(8,128)(2,1)S(1)} %slice.510) | copy-start | bytes 49156
  81.4 13.8 %copy-start.22 = (bf16[32,1,256]{2,0,1:T(8,128)(2,1)}, bf16[32,1,256]{2,0,1:T(8,128)(2,1)S(1)}, u32[]{:S(2)}) copy-start(bf16[32,1,256]{2,0,1:T(8,128)(2,1)S(1)} %collective-permute-done.1) | copy-start | bytes 49156
  85.4 10.1 %copy-start.12 = (bf16[128,64]{1,0:T(8,128)(2,1)S(1)}, bf16[128,64]{1,0:T(8,128)(2,1)}, u32[]{:S(2)}) copy-start(bf16[128,64]{1,0:T(8,128)(2,1)} %copy-done.11) | copy-start | bytes 49156
  85.4 8.3 %collective-permute-start.4 = (bf16[32,1,256]{2,0,1:T(8,128)(2,1)S(1)}, bf16[32,1,256]{2,0,1:T(8,128)(2,1)S(1)}, u32[]{:S(2)}, u32[]{:S(2)}) collective-permute-start(bf16[32,1,256]{2,0,1:T(8,128)(2,1)S(1)} %get-tuple-element.64), channel_id=1, source_target_pairs={{0,2},{2,4},{4,6},{6,8},{8,10},{10,12},{12,14},{14,16},{16,18},{18... | collective-permute-start | bytes 49160 | tf_op jit(solution)/shard_map/ppermute | solution.py:18
  87.4 7.8 %collective-permute-start.5 = (bf16[32,1,256]{2,0,1:T(8,128)(2,1)S(1)}, bf16[32,1,256]{2,0,1:T(8,128)(2,1)S(1)}, u32[]{:S(2)}, u32[]{:S(2)}) collective-permute-start(bf16[32,1,256]{2,0,1:T(8,128)(2,1)S(1)} %get-tuple-element.65), channel_id=1, source_target_pairs={{2,0},{4,2},{6,4},{8,6},{10,8},{12,10},{14,12},{16,14},{18,16},{20... | collective-permute-start | bytes 49160 | tf_op jit(solution)/shard_map/ppermute | solution.py:20
  100.6 7.4 %collective-permute-start.6 = (bf16[32,1,256]{2,0,1:T(8,128)(2,1)}, bf16[32,1,256]{2,0,1:T(8,128)(2,1)}, u32[]{:S(2)}, u32[]{:S(2)}) collective-permute-start(bf16[32,1,256]{2,0,1:T(8,128)(2,1)} %get-tuple-element.62), channel_id=1, source_target_pairs={{0,2},{2,4},{4,6},{6,8},{8,10},{10,12},{12,14},{14,16},{16,18},{18... | collective-permute-start | bytes 49160 | tf_op jit(solution)/shard_map/ppermute | solution.py:18
  102.5 6.4 %collective-permute-start.7 = (bf16[32,1,256]{2,0,1:T(8,128)(2,1)}, bf16[32,1,256]{2,0,1:T(8,128)(2,1)}, u32[]{:S(2)}, u32[]{:S(2)}) collective-permute-start(bf16[32,1,256]{2,0,1:T(8,128)(2,1)} %get-tuple-element.63), channel_id=1, source_target_pairs={{2,0},{4,2},{6,4},{8,6},{10,8},{12,10},{14,12},{16,14},{18,16},{20... | collective-permute-start | bytes 49160 | tf_op jit(solution)/shard_map/ppermute | solution.py:20
  116.3 11.3 %collective-permute-start.8 = (bf16[128,1,256]{2,0,1:T(8,128)(2,1)S(1)}, bf16[128,1,256]{2,0,1:T(8,128)(2,1)S(1)}, u32[]{:S(2)}, u32[]{:S(2)}) collective-permute-start(bf16[128,1,256]{2,0,1:T(8,128)(2,1)S(1)} %get-tuple-element.48), channel_id=1, source_target_pairs={{0,2},{2,4},{4,6},{6,8},{8,10},{10,12},{12,14},{14,16},{16,18},{18... | collective-permute-start | bytes 196616 | tf_op jit(solution)/shard_map/ppermute | solution.py:18
  118.3 9.4 %collective-permute-start.9 = (bf16[128,1,256]{2,0,1:T(8,128)(2,1)S(1)}, bf16[128,1,256]{2,0,1:T(8,128)(2,1)S(1)}, u32[]{:S(2)}, u32[]{:S(2)}) collective-permute-start(bf16[128,1,256]{2,0,1:T(8,128)(2,1)S(1)} %get-tuple-element.49), channel_id=1, source_target_pairs={{2,0},{4,2},{6,4},{8,6},{10,8},{12,10},{14,12},{16,14},{18,16},{20... | collective-permute-start | bytes 196616 | tf_op jit(solution)/shard_map/ppermute | solution.py:20
  133.2 9.2 %collective-permute-start.10 = (bf16[128,1,256]{2,0,1:T(8,128)(2,1)S(1)}, bf16[128,1,256]{2,0,1:T(8,128)(2,1)S(1)}, u32[]{:S(2)}, u32[]{:S(2)}) collective-permute-start(bf16[128,1,256]{2,0,1:T(8,128)(2,1)S(1)} %get-tuple-element.46), channel_id=1, source_target_pairs={{0,2},{2,4},{4,6},{6,8},{8,10},{10,12},{12,14},{14,16},{16,18},{18... | collective-permute-start | bytes 196616 | tf_op jit(solution)/shard_map/ppermute | solution.py:18
  135.1 7.3 %collective-permute-start.11 = (bf16[128,1,256]{2,0,1:T(8,128)(2,1)S(1)}, bf16[128,1,256]{2,0,1:T(8,128)(2,1)S(1)}, u32[]{:S(2)}, u32[]{:S(2)}) collective-permute-start(bf16[128,1,256]{2,0,1:T(8,128)(2,1)S(1)} %get-tuple-element.47), channel_id=1, source_target_pairs={{2,0},{4,2},{6,4},{8,6},{10,8},{12,10},{14,12},{16,14},{18,16},{20... | collective-permute-start | bytes 196616 | tf_op jit(solution)/shard_map/ppermute | solution.py:20
  148.1 11.4 %collective-permute-start.12 = (bf16[128,1,256]{2,0,1:T(8,128)(2,1)S(1)}, bf16[128,1,256]{2,0,1:T(8,128)(2,1)S(1)}, u32[]{:S(2)}, u32[]{:S(2)}) collective-permute-start(bf16[128,1,256]{2,0,1:T(8,128)(2,1)S(1)} %get-tuple-element.44), channel_id=1, source_target_pairs={{0,2},{2,4},{4,6},{6,8},{8,10},{10,12},{12,14},{14,16},{16,18},{18... | collective-permute-start | bytes 196616 | tf_op jit(solution)/shard_map/ppermute | solution.py:18
  150.0 9.5 %collective-permute-start.13 = (bf16[128,1,256]{2,0,1:T(8,128)(2,1)S(1)}, bf16[128,1,256]{2,0,1:T(8,128)(2,1)S(1)}, u32[]{:S(2)}, u32[]{:S(2)}) collective-permute-start(bf16[128,1,256]{2,0,1:T(8,128)(2,1)S(1)} %get-tuple-element.45), channel_id=1, source_target_pairs={{2,0},{4,2},{6,4},{8,6},{10,8},{12,10},{14,12},{16,14},{18,16},{20... | collective-permute-start | bytes 196616 | tf_op jit(solution)/shard_map/ppermute | solution.py:20
  (20 other events, 27.3 us)
Sparse Core Ops, SparseCore 0:
  159.6 128.1 all-reduce.8
where the time goes:
time: 297 us; the launch traced here: 296 us
  blocking collectives  92.8 us (31%)
  waiting for transfers between devices  84.2 us (28%)
  starting transfers between devices  49.7 us (17%)
  matrix products  27.1 us (9%)
  local copies, waits for them, and re-layouts  16 us (5%)
  between operations  15 us (5%)
  other arithmetic  11 us (4%)
    unnamed x2, waiting for transfers between devices  81.9 us
    all_gather x1, blocking collectives, per_device(): lax.all_gather(gate_weights, ('rows', 'maze'), axis=0, tiled=True)  53.3 us
    psum x1, blocking collectives, per_device(): grad_table = lax.psum(pieces, ('rows', 'maze')) * scale  39.5 us
    ppermute x7, starting transfers between devices, extended(): lax.ppermute(head, axis, [((i + 1) % count, i) for i in range(ends)])  36.2 us
    ppermute x7, starting transfers between devices, extended(): lax.ppermute(tail, axis, [(i, (i + 1) % count) for i in range(ends)])  13.4 us
    unnamed x63, local copies, waits for them, and re-layouts  9.98 us
    dot_general x27, matrix products, gate_conv(): jnp.einsum('gc,crq->grq', kernel[tap_index], window, preferred_element_ty...  9.61 us
    dot_general x27, matrix products, weight_grads(): jnp.einsum('grq,crq->gc', gate_grad, window, preferred_element_type=jnp.f...  8.87 us
  transfers between devices with their start and end apart: 15, of which 3 were waited for; matrix products, arithmetic and copies ran while one was open for 7% of the time, Pallas kernels for 0%

commit v1 on v0

--- a/solution.py
+++ b/solution.py
@@ -141,7 +141,7 @@
             jnp.sum(input_acc * goal_bump, axis=(1, 2)),
         ]
     )
-    grad_table = lax.psum(pieces, ("rows", "maze")) * scale
+    grad_table = jnp.sum(lax.all_gather(pieces, ("rows", "maze")), axis=0) * scale
     return (grad_weights, grad_table, carry_hidden[None], carry_cell[None])
 
 

time: 297 us -> 297 us (level)
  blocking collectives: 92.8 us -> 106 us
  waiting for transfers between devices: 84.2 us -> 71.4 us
    all_gather x0 -> x1, blocking collectives: none -> 52.3 us  [per_device(): lax.all_gather(pieces, ('rows', 'maze'))]
    psum x1 -> x0, blocking collectives: 39.5 us -> none  [per_device(): grad_table = lax.psum(pieces, ('rows', 'maze')) * scale]
    unnamed x2, waiting for transfers between devices: 81.9 us -> 69 us
where the time goes in v1:
time: 297 us; the launch traced here: 296 us
  blocking collectives  106 us (36%)
  waiting for transfers between devices  71.4 us (24%)
  starting transfers between devices  49.7 us (17%)
  matrix products  27.1 us (9%)
  local copies, waits for them, and re-layouts  16 us (5%)
  between operations  15 us (5%)
  other arithmetic  11.1 us (4%)
    unnamed x2, waiting for transfers between devices  69 us
    all_gather x1, blocking collectives, per_device(): lax.all_gather(gate_weights, ('rows', 'maze'), axis=0, tiled=True)  53.3 us
    all_gather x1, blocking collectives, per_device(): lax.all_gather(pieces, ('rows', 'maze'))  52.3 us
    ppermute x7, starting transfers between devices, extended(): lax.ppermute(head, axis, [((i + 1) % count, i) for i in range(ends)])  36.2 us
    ppermute x7, starting transfers between devices, extended(): lax.ppermute(tail, axis, [(i, (i + 1) % count) for i in range(ends)])  13.4 us
    unnamed x63, local copies, waits for them, and re-layouts  9.98 us
    dot_general x27, matrix products, gate_conv(): jnp.einsum('gc,crq->grq', kernel[tap_index], window, preferred_element_ty...  9.61 us
    dot_general x27, matrix products, weight_grads(): jnp.einsum('grq,crq->gc', gate_grad, window, preferred_element_type=jnp.f...  8.87 us
  transfers between devices with their start and end apart: 15, of which 3 were waited for; matrix products, arithmetic and copies ran while one was open for 7% of the time, Pallas kernels for 0%

profile of v1, /device:TPU:8, one launch (start us, length us, event | category | flops | bytes accessed | tf_op | source)
XLA Modules:
  0.0 295.9 jit_solution(204797417117700422)
XLA Ops:
  7.2 1.3 fusion.286
  11.6 1.9 collective-permute-start
  13.5 4.5 %collective-permute-start.1 = (bf16[32,1,256]{2,0,1:T(8,128)(2,1)S(1)}, bf16[32,1,256]{2,0,1:T(8,128)(2,1)S(1)}, u32[]{:S(2)}, u32[]{:S(2)}) collective-permute-start(bf16[32,1,256]{2,0,1:T(8,128)(2,1)S(1)} %get-tuple-element.67), channel_id=1, source_target_pairs={{2,0},{4,2},{6,4},{8,6},{10,8},{12,10},{14,12},{16,14},{18,16},{20... | collective-permute-start | bytes 49160 | tf_op jit(solution)/shard_map/ppermute | solution.py:20
  19.0 1.9 collective-permute-start.2
  20.9 4.5 %collective-permute-start.3 = (bf16[32,1,256]{2,0,1:T(8,128)(2,1)S(1)}, bf16[32,1,256]{2,0,1:T(8,128)(2,1)S(1)}, u32[]{:S(2)}, u32[]{:S(2)}) collective-permute-start(bf16[32,1,256]{2,0,1:T(8,128)(2,1)S(1)} %get-tuple-element.69), channel_id=1, source_target_pairs={{2,0},{4,2},{6,4},{8,6},{10,8},{12,10},{14,12},{16,14},{18,16},{20... | collective-permute-start | bytes 49160 | tf_op jit(solution)/shard_map/ppermute | solution.py:20
  26.2 53.3 %all-gather.1 = bf16[32,1,2304]{2,1,0:T(2,128)(2,1)S(1)} all-gather(bf16[1,1,2304]{2,1,0:T(2,128)(2,1)S(1)} %reshape.145), channel_id=1, replica_groups=mesh['rows'=16,'maze'=2] {'rows','maze'}, dimensions={0}, use_global_device_ids=true | all-gather | bytes 152064 | tf_op jit(solution)/shard_map/all_gather | solution.py:65
  85.4 1.9 collective-permute-start.4
  87.4 6.4 %collective-permute-start.5 = (bf16[32,1,256]{2,0,1:T(8,128)(2,1)S(1)}, bf16[32,1,256]{2,0,1:T(8,128)(2,1)S(1)}, u32[]{:S(2)}, u32[]{:S(2)}) collective-permute-start(bf16[32,1,256]{2,0,1:T(8,128)(2,1)S(1)} %get-tuple-element.65), channel_id=1, source_target_pairs={{2,0},{4,2},{6,4},{8,6},{10,8},{12,10},{14,12},{16,14},{18,16},{20... | collective-permute-start | bytes 49160 | tf_op jit(solution)/shard_map/ppermute | solution.py:20
  93.8 1.4 collective-permute-done.5
  98.3 0.9 multiply_convert_fusion.10
  99.2 1.3 fusion.282
  100.6 1.9 collective-permute-start.6
  102.5 4.7 %collective-permute-start.7 = (bf16[32,1,256]{2,0,1:T(8,128)(2,1)}, bf16[32,1,256]{2,0,1:T(8,128)(2,1)}, u32[]{:S(2)}, u32[]{:S(2)}) collective-permute-start(bf16[32,1,256]{2,0,1:T(8,128)(2,1)} %get-tuple-element.63), channel_id=1, source_target_pairs={{2,0},{4,2},{6,4},{8,6},{10,8},{12,10},{14,12},{16,14},{18,16},{20... | collective-permute-start | bytes 49160 | tf_op jit(solution)/shard_map/ppermute | solution.py:20
  108.8 0.9 maximum_maximum_fusion.2
  109.8 1.1 fusion.180
  116.3 1.9 collective-permute-start.8
  118.3 6.7 %collective-permute-start.9 = (bf16[128,1,256]{2,0,1:T(8,128)(2,1)S(1)}, bf16[128,1,256]{2,0,1:T(8,128)(2,1)S(1)}, u32[]{:S(2)}, u32[]{:S(2)}) collective-permute-start(bf16[128,1,256]{2,0,1:T(8,128)(2,1)S(1)} %get-tuple-element.49), channel_id=1, source_target_pairs={{2,0},{4,2},{6,4},{8,6},{10,8},{12,10},{14,12},{16,14},{18,16},{20... | collective-permute-start | bytes 196616 | tf_op jit(solution)/shard_map/ppermute | solution.py:20
  133.2 1.9 collective-permute-start.10
  135.1 4.6 %collective-permute-start.11 = (bf16[128,1,256]{2,0,1:T(8,128)(2,1)S(1)}, bf16[128,1,256]{2,0,1:T(8,128)(2,1)S(1)}, u32[]{:S(2)}, u32[]{:S(2)}) collective-permute-start(bf16[128,1,256]{2,0,1:T(8,128)(2,1)S(1)} %get-tuple-element.47), channel_id=1, source_target_pairs={{2,0},{4,2},{6,4},{8,6},{10,8},{12,10},{14,12},{16,14},{18,16},{20... | collective-permute-start | bytes 196616 | tf_op jit(solution)/shard_map/ppermute | solution.py:20
  148.1 1.9 collective-permute-start.12
  150.0 4.8 %collective-permute-start.13 = (bf16[128,1,256]{2,0,1:T(8,128)(2,1)S(1)}, bf16[128,1,256]{2,0,1:T(8,128)(2,1)S(1)}, u32[]{:S(2)}, u32[]{:S(2)}) collective-permute-start(bf16[128,1,256]{2,0,1:T(8,128)(2,1)S(1)} %get-tuple-element.45), channel_id=1, source_target_pairs={{2,0},{4,2},{6,4},{8,6},{10,8},{12,10},{14,12},{16,14},{18,16},{20... | collective-permute-start | bytes 196616 | tf_op jit(solution)/shard_map/ppermute | solution.py:20
  165.7 52.3 %all-gather.2 = f32[32,3,32]{2,1,0:T(4,128)S(1)} all-gather(f32[1,3,32]{2,1,0:T(4,128)S(1)} %maximum_bitcast_fusion), channel_id=2, replica_groups=mesh['rows'=16,'maze'=2] {'rows','maze'}, dimensions={0}, use_global_device_ids=true | all-gather | bytes 12672 | tf_op jit(solution)/shard_map/all_gather | solution.py:144
  218.7 69.0 %all-reduce.9.cloned.1.call-done = f32[73728]{0:T(1024)} async-done(((f32[73728]{0:T(1024)}), f32[73728]{0:T(1024)}) %all-reduce.9.cloned.1.call-update) | async-done | bytes 294928
  287.7 1.4 dynamic-slice_multiply_fusion
  (203 shorter events, 48.2 us)
Async XLA Ops:
  7.2 280.5 %all-reduce.9.cloned.1.call-start = ((), (), s32[]{:S(2)}) async-start(), calls=%async_computation | async-start | bytes 589824
  10.7 14.8 %copy-start.25 = (f32[8,256]{1,0:T(8,128)}, f32[8,256]{1,0:T(8,128)S(1)}, u32[]{:S(2)}) copy-start(f32[8,256]{1,0:T(8,128)S(1)} %get-tuple-element.30) | copy-start | bytes 24580
  10.7 14.8 %copy-start.23 = (f32[8,256]{1,0:T(8,128)}, f32[8,256]{1,0:T(8,128)S(1)}, u32[]{:S(2)}) copy-start(f32[8,256]{1,0:T(8,128)S(1)} %convert_bitcast_fusion) | copy-start | bytes 24580
  11.4 14.1 %copy-start.27 = (f32[8,256]{1,0:T(8,128)}, f32[8,256]{1,0:T(8,128)S(1)}, u32[]{:S(2)}) copy-start(f32[8,256]{1,0:T(8,128)S(1)} %multiply_exponential_fusion) | copy-start | bytes 24580
  11.6 69.8 %collective-permute-start = (bf16[32,1,256]{2,0,1:T(8,128)(2,1)S(1)}, bf16[32,1,256]{2,0,1:T(8,128)(2,1)S(1)}, u32[]{:S(2)}, u32[]{:S(2)}) collective-permute-start(bf16[32,1,256]{2,0,1:T(8,128)(2,1)S(1)} %get-tuple-element.66), channel_id=1, source_target_pairs={{0,2},{2,4},{4,6},{6,8},{8,10},{10,12},{12,14},{14,16},{16,18},{18... | collective-permute-start | bytes 49160 | tf_op jit(solution)/shard_map/ppermute | solution.py:18
  13.5 67.9 %collective-permute-start.1 = (bf16[32,1,256]{2,0,1:T(8,128)(2,1)S(1)}, bf16[32,1,256]{2,0,1:T(8,128)(2,1)S(1)}, u32[]{:S(2)}, u32[]{:S(2)}) collective-permute-start(bf16[32,1,256]{2,0,1:T(8,128)(2,1)S(1)} %get-tuple-element.67), channel_id=1, source_target_pairs={{2,0},{4,2},{6,4},{8,6},{10,8},{12,10},{14,12},{16,14},{18,16},{20... | collective-permute-start | bytes 49160 | tf_op jit(solution)/shard_map/ppermute | solution.py:20
  19.0 62.4 %collective-permute-start.2 = (bf16[32,1,256]{2,0,1:T(8,128)(2,1)S(1)}, bf16[32,1,256]{2,0,1:T(8,128)(2,1)S(1)}, u32[]{:S(2)}, u32[]{:S(2)}) collective-permute-start(bf16[32,1,256]{2,0,1:T(8,128)(2,1)S(1)} %get-tuple-element.68), channel_id=1, source_target_pairs={{0,2},{2,4},{4,6},{6,8},{8,10},{10,12},{12,14},{14,16},{16,18},{18... | collective-permute-start | bytes 49160 | tf_op jit(solution)/shard_map/ppermute | solution.py:18
  20.9 60.5 %collective-permute-start.3 = (bf16[32,1,256]{2,0,1:T(8,128)(2,1)S(1)}, bf16[32,1,256]{2,0,1:T(8,128)(2,1)S(1)}, u32[]{:S(2)}, u32[]{:S(2)}) collective-permute-start(bf16[32,1,256]{2,0,1:T(8,128)(2,1)S(1)} %get-tuple-element.69), channel_id=1, source_target_pairs={{2,0},{4,2},{6,4},{8,6},{10,8},{12,10},{14,12},{16,14},{18,16},{20... | collective-permute-start | bytes 49160 | tf_op jit(solution)/shard_map/ppermute | solution.py:20
  80.8 16.8 %copy-start.7 = (bf16[128,64]{1,0:T(8,128)(2,1)}, bf16[128,64]{1,0:T(8,128)(2,1)S(1)}, u32[]{:S(2)}) copy-start(bf16[128,64]{1,0:T(8,128)(2,1)S(1)} %slice.531) | copy-start | bytes 49156
  81.0 15.6 %copy-start.9 = (bf16[128,64]{1,0:T(8,128)(2,1)}, bf16[128,64]{1,0:T(8,128)(2,1)S(1)}, u32[]{:S(2)}) copy-start(bf16[128,64]{1,0:T(8,128)(2,1)S(1)} %slice.522) | copy-start | bytes 49156
  81.2 14.7 %copy-start = (bf16[128,64]{1,0:T(8,128)(2,1)}, bf16[128,64]{1,0:T(8,128)(2,1)S(1)}, u32[]{:S(2)}) copy-start(bf16[128,64]{1,0:T(8,128)(2,1)S(1)} %slice.516) | copy-start | bytes 49156
  81.4 13.8 %copy-start.2 = (bf16[128,64]{1,0:T(8,128)(2,1)}, bf16[128,64]{1,0:T(8,128)(2,1)S(1)}, u32[]{:S(2)}) copy-start(bf16[128,64]{1,0:T(8,128)(2,1)S(1)} %slice.510) | copy-start | bytes 49156
  81.4 13.8 %copy-start.22 = (bf16[32,1,256]{2,0,1:T(8,128)(2,1)}, bf16[32,1,256]{2,0,1:T(8,128)(2,1)S(1)}, u32[]{:S(2)}) copy-start(bf16[32,1,256]{2,0,1:T(8,128)(2,1)S(1)} %collective-permute-done.1) | copy-start | bytes 49156
  85.4 10.1 %copy-start.12 = (bf16[128,64]{1,0:T(8,128)(2,1)S(1)}, bf16[128,64]{1,0:T(8,128)(2,1)}, u32[]{:S(2)}) copy-start(bf16[128,64]{1,0:T(8,128)(2,1)} %copy-done.11) | copy-start | bytes 49156
  85.4 8.3 %collective-permute-start.4 = (bf16[32,1,256]{2,0,1:T(8,128)(2,1)S(1)}, bf16[32,1,256]{2,0,1:T(8,128)(2,1)S(1)}, u32[]{:S(2)}, u32[]{:S(2)}) collective-permute-start(bf16[32,1,256]{2,0,1:T(8,128)(2,1)S(1)} %get-tuple-element.64), channel_id=1, source_target_pairs={{0,2},{2,4},{4,6},{6,8},{8,10},{10,12},{12,14},{14,16},{16,18},{18... | collective-permute-start | bytes 49160 | tf_op jit(solution)/shard_map/ppermute | solution.py:18
  87.4 7.8 %collective-permute-start.5 = (bf16[32,1,256]{2,0,1:T(8,128)(2,1)S(1)}, bf16[32,1,256]{2,0,1:T(8,128)(2,1)S(1)}, u32[]{:S(2)}, u32[]{:S(2)}) collective-permute-start(bf16[32,1,256]{2,0,1:T(8,128)(2,1)S(1)} %get-tuple-element.65), channel_id=1, source_target_pairs={{2,0},{4,2},{6,4},{8,6},{10,8},{12,10},{14,12},{16,14},{18,16},{20... | collective-permute-start | bytes 49160 | tf_op jit(solution)/shard_map/ppermute | solution.py:20
  100.6 7.4 %collective-permute-start.6 = (bf16[32,1,256]{2,0,1:T(8,128)(2,1)}, bf16[32,1,256]{2,0,1:T(8,128)(2,1)}, u32[]{:S(2)}, u32[]{:S(2)}) collective-permute-start(bf16[32,1,256]{2,0,1:T(8,128)(2,1)} %get-tuple-element.62), channel_id=1, source_target_pairs={{0,2},{2,4},{4,6},{6,8},{8,10},{10,12},{12,14},{14,16},{16,18},{18... | collective-permute-start | bytes 49160 | tf_op jit(solution)/shard_map/ppermute | solution.py:18
  102.5 6.4 %collective-permute-start.7 = (bf16[32,1,256]{2,0,1:T(8,128)(2,1)}, bf16[32,1,256]{2,0,1:T(8,128)(2,1)}, u32[]{:S(2)}, u32[]{:S(2)}) collective-permute-start(bf16[32,1,256]{2,0,1:T(8,128)(2,1)} %get-tuple-element.63), channel_id=1, source_target_pairs={{2,0},{4,2},{6,4},{8,6},{10,8},{12,10},{14,12},{16,14},{18,16},{20... | collective-permute-start | bytes 49160 | tf_op jit(solution)/shard_map/ppermute | solution.py:20
  116.3 11.3 %collective-permute-start.8 = (bf16[128,1,256]{2,0,1:T(8,128)(2,1)S(1)}, bf16[128,1,256]{2,0,1:T(8,128)(2,1)S(1)}, u32[]{:S(2)}, u32[]{:S(2)}) collective-permute-start(bf16[128,1,256]{2,0,1:T(8,128)(2,1)S(1)} %get-tuple-element.48), channel_id=1, source_target_pairs={{0,2},{2,4},{4,6},{6,8},{8,10},{10,12},{12,14},{14,16},{16,18},{18... | collective-permute-start | bytes 196616 | tf_op jit(solution)/shard_map/ppermute | solution.py:18
  118.3 9.4 %collective-permute-start.9 = (bf16[128,1,256]{2,0,1:T(8,128)(2,1)S(1)}, bf16[128,1,256]{2,0,1:T(8,128)(2,1)S(1)}, u32[]{:S(2)}, u32[]{:S(2)}) collective-permute-start(bf16[128,1,256]{2,0,1:T(8,128)(2,1)S(1)} %get-tuple-element.49), channel_id=1, source_target_pairs={{2,0},{4,2},{6,4},{8,6},{10,8},{12,10},{14,12},{16,14},{18,16},{20... | collective-permute-start | bytes 196616 | tf_op jit(solution)/shard_map/ppermute | solution.py:20
  133.2 9.2 %collective-permute-start.10 = (bf16[128,1,256]{2,0,1:T(8,128)(2,1)S(1)}, bf16[128,1,256]{2,0,1:T(8,128)(2,1)S(1)}, u32[]{:S(2)}, u32[]{:S(2)}) collective-permute-start(bf16[128,1,256]{2,0,1:T(8,128)(2,1)S(1)} %get-tuple-element.46), channel_id=1, source_target_pairs={{0,2},{2,4},{4,6},{6,8},{8,10},{10,12},{12,14},{14,16},{16,18},{18... | collective-permute-start | bytes 196616 | tf_op jit(solution)/shard_map/ppermute | solution.py:18
  135.1 7.3 %collective-permute-start.11 = (bf16[128,1,256]{2,0,1:T(8,128)(2,1)S(1)}, bf16[128,1,256]{2,0,1:T(8,128)(2,1)S(1)}, u32[]{:S(2)}, u32[]{:S(2)}) collective-permute-start(bf16[128,1,256]{2,0,1:T(8,128)(2,1)S(1)} %get-tuple-element.47), channel_id=1, source_target_pairs={{2,0},{4,2},{6,4},{8,6},{10,8},{12,10},{14,12},{16,14},{18,16},{20... | collective-permute-start | bytes 196616 | tf_op jit(solution)/shard_map/ppermute | solution.py:20
  148.1 11.4 %collective-permute-start.12 = (bf16[128,1,256]{2,0,1:T(8,128)(2,1)S(1)}, bf16[128,1,256]{2,0,1:T(8,128)(2,1)S(1)}, u32[]{:S(2)}, u32[]{:S(2)}) collective-permute-start(bf16[128,1,256]{2,0,1:T(8,128)(2,1)S(1)} %get-tuple-element.44), channel_id=1, source_target_pairs={{0,2},{2,4},{4,6},{6,8},{8,10},{10,12},{12,14},{14,16},{16,18},{18... | collective-permute-start | bytes 196616 | tf_op jit(solution)/shard_map/ppermute | solution.py:18
  150.0 9.5 %collective-permute-start.13 = (bf16[128,1,256]{2,0,1:T(8,128)(2,1)S(1)}, bf16[128,1,256]{2,0,1:T(8,128)(2,1)S(1)}, u32[]{:S(2)}, u32[]{:S(2)}) collective-permute-start(bf16[128,1,256]{2,0,1:T(8,128)(2,1)S(1)} %get-tuple-element.45), channel_id=1, source_target_pairs={{2,0},{4,2},{6,4},{8,6},{10,8},{12,10},{14,12},{16,14},{18,16},{20... | collective-permute-start | bytes 196616 | tf_op jit(solution)/shard_map/ppermute | solution.py:20
  (20 other events, 27.3 us)
Sparse Core Ops, SparseCore 0:
  159.6 128.0 all-reduce.8
